TPU v7x, 32 devices: a whole 2x2x4 slice. The times are simulated.
32 devices in a mesh: gz: 2 (over x), gy: 4 (over z), gx: 4 (over y, core).
Axes of the slice: x: 2, y: 2, z: 4, core: 2. Of those that a mesh axis runs over, the one named last changes fastest.
Arguments:
- density: float32 [16, 32, 512], P('gz', 'gy', 'gx'), may hold values from 0.3 to 3
- velocity: float32 [3, 16, 32, 512], P(None, 'gz', 'gy', 'gx'), may hold values from -3 to 3
- pressure: float32 [16, 32, 512], P('gz', 'gy', 'gx'), may hold values from 0.3 to 3
- field: float32 [3, 16, 32, 512], P(None, 'gz', 'gy', 'gx'), may hold values from -3 to 3
- corona: int32 [16], replicated, may hold values from 0 to 1, as said below
Outputs:
- conserved: float32 [5, 16, 32, 512], P(None, 'gz', 'gy', 'gx')
- faces_new: float32 [3, 16, 32, 512], P(None, 'gz', 'gy', 'gx')
Inputs may be any that keep to these rules, and one draw needn't show every extreme that they name: `corona`: 1 marks a cooled slab; every slab farther from the midplane than a drawn height (one for each half of z) is cooled, and some other slabs are cooled too.
All inputs are finite; a program needn't handle non-finite values.
Results may differ from a plain program's by a relative error of at most 0.00002.
Values sent between devices are 32-bit elements; how exact they have to be, the bound alone decides.
A program may use at most 64 MiB of HBM per device.

v0:
```python
import jax
import jax.numpy as jnp
from jax import lax
from jax.sharding import PartitionSpec as P

COOL_STEPS = 8


adiabatic = 5.0 / 3.0
courant = 0.08
cool_rate = 0.03
gravity = 1.0
cyclic_pairs = ((2, 1), (0, 2), (1, 0))


def with_halo(cells, sides, width, closed):
    for axis, dim in sides:
        count = lax.axis_size(axis)
        ends = count if closed else count - 1
        head = lax.slice_in_dim(cells, 0, width, axis=dim)
        tail = lax.slice_in_dim(cells, cells.shape[dim] - width, cells.shape[dim], axis=dim)
        cells = jnp.concatenate(
            [
                lax.ppermute(tail, axis, [(i, (i + 1) % count) for i in range(ends)]),
                cells,
                lax.ppermute(head, axis, [((i + 1) % count, i) for i in range(ends)]),
            ],
            axis=dim,
        )
    return cells


def shift_up(values, along):
    return jnp.roll(values, -1, along)


def shift_down(values, along):
    return jnp.roll(values, 1, along)


def cool_cells(density, pressure):
    for subcycle in range(COOL_STEPS):
        pressure = pressure / (1.0 + cool_rate * jnp.sqrt(density * pressure))
    return pressure


def cool_marked(density, pressure, marks):
    return jnp.where(marks[:, None, None] == 1, cool_cells(density, pressure), pressure)


def state_terms(density, velocity, pressure, magnetic, normal_axis):
    others = [component for component in range(3) if component != normal_axis]
    normal_field = magnetic[normal_axis]
    transverse = (
        magnetic[others[0]] * magnetic[others[0]] + magnetic[others[1]] * magnetic[others[1]]
    )
    squared = transverse + normal_field * normal_field
    total_pressure = pressure + 0.5 * squared
    kinetic = velocity[0] * velocity[0] + velocity[1] * velocity[1] + velocity[2] * velocity[2]
    alignment = velocity[0] * magnetic[0] + velocity[1] * magnetic[1] + velocity[2] * magnetic[2]
    energy = pressure / (adiabatic - 1.0) + 0.5 * density * kinetic + 0.5 * squared
    sound = adiabatic * pressure / density
    along_field = normal_field * normal_field / density
    across_field = transverse / density
    fast_speed = jnp.sqrt(
        0.5
        * (
            sound
            + along_field
            + across_field
            + jnp.sqrt((sound - along_field - across_field) ** 2 + 4.0 * sound * across_field)
        )
    )
    normal_speed = velocity[normal_axis]
    conserved = (
        [density]
        + [density * velocity[component] for component in range(3)]
        + [energy]
        + [magnetic[component] for component in others]
    )
    fluxes = [density * normal_speed]
    for component in range(3):
        moment = density * velocity[component] * normal_speed - magnetic[component] * normal_field
        if component == normal_axis:
            moment = moment + total_pressure
        fluxes.append(moment)
    fluxes.append((energy + total_pressure) * normal_speed - normal_field * alignment)
    for component in others:
        fluxes.append(normal_speed * magnetic[component] - velocity[component] * normal_field)
    return (normal_speed, fast_speed, conserved, fluxes)


def interface_flux(density, velocity, pressure, centre, normal_face, normal_axis):
    lower_field = [shift_down(member, normal_axis) for member in centre]
    lower_field[normal_axis] = normal_face
    upper_field = list(centre)
    upper_field[normal_axis] = normal_face
    lower_terms = state_terms(
        shift_down(density, normal_axis),
        [shift_down(member, normal_axis) for member in velocity],
        shift_down(pressure, normal_axis),
        lower_field,
        normal_axis,
    )
    upper_terms = state_terms(density, velocity, pressure, upper_field, normal_axis)
    slowest = jnp.minimum(
        jnp.minimum(lower_terms[0] - lower_terms[1], upper_terms[0] - upper_terms[1]), 0.0
    )
    fastest = jnp.maximum(
        jnp.maximum(lower_terms[0] + lower_terms[1], upper_terms[0] + upper_terms[1]), 0.0
    )
    inverse = 1.0 / (fastest - slowest)
    result = []
    for member in range(7):
        lower_flux = lower_terms[3][member]
        upper_flux = upper_terms[3][member]
        jump = upper_terms[2][member] - lower_terms[2][member]
        result.append(
            (fastest * lower_flux - slowest * upper_flux + slowest * fastest * jump) * inverse
        )
    return result


def advance(extended, height):
    density = extended[0]
    velocity = [extended[1], extended[2], extended[3]]
    pressure = extended[4]
    faces = [extended[5], extended[6], extended[7]]
    centre = [
        0.5 * (faces[component] + shift_up(faces[component], component)) for component in range(3)
    ]
    fluxes = [
        interface_flux(density, velocity, pressure, centre, faces[direction], direction)
        for direction in range(3)
    ]
    kinetic = velocity[0] * velocity[0] + velocity[1] * velocity[1] + velocity[2] * velocity[2]
    squared = centre[0] * centre[0] + centre[1] * centre[1] + centre[2] * centre[2]
    energy = pressure / (adiabatic - 1.0) + 0.5 * density * kinetic + 0.5 * squared
    conserved = [
        density,
        density * velocity[0],
        density * velocity[1],
        density * velocity[2],
        energy,
    ]
    inner = (slice(2, -2), slice(2, -2), slice(2, -2))
    updated = []
    for member in range(5):
        change = jnp.zeros_like(density)
        for direction in range(3):
            change = (
                change + shift_up(fluxes[direction][member], direction) - fluxes[direction][member]
            )
        updated.append((conserved[member] - courant * change)[inner])
    pull = -gravity * height[:, None, None]
    updated[1] = updated[1] + courant * density[inner] * pull
    updated[4] = updated[4] + courant * density[inner] * velocity[0][inner] * pull
    electric = []
    for edge in range(3):
        first, second = cyclic_pairs[edge]
        first_others = [component for component in range(3) if component != first]
        second_others = [component for component in range(3) if component != second]
        first_flux = fluxes[first][5 + first_others.index(second)]
        second_flux = fluxes[second][5 + second_others.index(first)]
        electric.append(
            0.25
            * (
                second_flux
                + shift_down(second_flux, first)
                - first_flux
                - shift_down(first_flux, second)
            )
        )
    new_faces = []
    for component in range(3):
        across, beyond = cyclic_pairs[component]
        curl = (
            shift_up(electric[beyond], across)
            - electric[beyond]
            - (shift_up(electric[across], beyond) - electric[across])
        )
        new_faces.append((faces[component] - courant * curl)[inner])
    return (jnp.stack(updated), jnp.stack(new_faces))


def clamp_dim(extended, dim, at_lower, at_upper):
    length = extended.shape[dim]
    lower_edge = lax.slice_in_dim(extended, 2, 3, axis=dim)
    upper_edge = lax.slice_in_dim(extended, length - 3, length - 2, axis=dim)
    lower_rims = jnp.where(
        at_lower,
        jnp.concatenate([lower_edge, lower_edge], dim),
        lax.slice_in_dim(extended, 0, 2, axis=dim),
    )
    upper_rims = jnp.where(
        at_upper,
        jnp.concatenate([upper_edge, upper_edge], dim),
        lax.slice_in_dim(extended, length - 2, length, axis=dim),
    )
    middle = lax.slice_in_dim(extended, 2, length - 2, axis=dim)
    return jnp.concatenate([lower_rims, middle, upper_rims], dim)


def rim_across_x(stacked):
    return with_halo(stacked, (("gx", 3),), 2, True)


def rim_across_yz(stacked):
    extended = with_halo(stacked, (("gz", 1), ("gy", 2)), 2, False)
    row_index = lax.axis_index("gy")
    extended = clamp_dim(extended, 2, row_index == 0, row_index == lax.axis_size("gy") - 1)
    slab_index = lax.axis_index("gz")
    return clamp_dim(extended, 1, slab_index == 0, slab_index == lax.axis_size("gz") - 1)


def on_device(density, velocity, pressure, field, corona):
    slabs = density.shape[0]
    slab_index = lax.axis_index("gz")
    marks = lax.dynamic_slice_in_dim(corona, slab_index * slabs, slabs)
    cooled = cool_marked(density, pressure, marks)
    stacked = jnp.concatenate([density[None], velocity, cooled[None], field], 0)
    extended = rim_across_x(rim_across_yz(stacked))
    total_slabs = slabs * lax.axis_size("gz")
    global_slab = slab_index * slabs + jnp.arange(slabs, dtype=jnp.int32)
    height = (2 * global_slab + 1 - total_slabs).astype(jnp.float32) / total_slabs
    return advance(extended, height)


def solution(mesh):
    return jax.shard_map(
        on_device,
        mesh=mesh,
        in_specs=(
            P("gz", "gy", "gx"),
            P(None, "gz", "gy", "gx"),
            P("gz", "gy", "gx"),
            P(None, "gz", "gy", "gx"),
            P(),
        ),
        out_specs=(P(None, "gz", "gy", "gx"), P(None, "gz", "gy", "gx")),
        check_vma=False,
    )
```

profile of v0, /device:TPU:0, one launch (start us, length us, event | category | flops | bytes accessed | tf_op | source)
XLA Modules:
  0.0 48.3 jit_solution(2420380765245593263)
XLA Ops:
  0.7 0.8 %dynamic-slice_compare_fusion = pred[8]{0:T(512)(128)(4,1)S(1)} fusion(s32[16]{0:T(128)} %param.9, s32[]{:T(128)S(6)} %select_n.37), kind=kLoop, calls=%fused_computation.239 | loop fusion | flops 8 | bytes 44 | tf_op jit(solution)/shard_map/eq | solution.py:48
  1.5 0.9 %fusion.21 = f32[1,8,8,128]{3,2,1,0:T(8,128)S(1)} fusion(f32[8,8,128]{2,1,0:T(8,128)} %param.7, f32[8,8,128]{2,1,0:T(8,128)} %param.5, pred[8]{0:T(512)(128)(4,1)S(1)} %dynamic-slice_compare_fusion), kind=kLoop, calls=%fused_computation.148 | loop fusion | flops 327680 | bytes 98312 | tf_op jit(solution)/shard_map/broadcast_in_dim | solution.py:221
  2.4 0.8 %pad_maximum_fusion.34 = (f32[8,2,8,128]{3,2,1,0:T(8,128)S(1)}, f32[8,2,8,128]{3,2,1,0:T(8,128)S(1)}) fusion(f32[3,8,8,128]{3,2,1,0:T(8,128)} %param.8, f32[1,8,8,128]{3,2,1,0:T(8,128)S(1)} %fusion.21, f32[3,8,8,128]{3,2,1,0:T(8,128)} %param.6, f32[1,8,8,128]{3,2,1,0:T(8,128)} %bitcast.335), kind=kLoop, calls=%fused_computation.144 | loop fusion | flops 98304 | bytes 393216 | tf_op jit(solution)/shard_map/slice | solution.py:21
  3.2 4.9 %collective-permute-start = (f32[8,2,8,128]{3,2,1,0:T(8,128)S(1)}, f32[8,2,8,128]{3,2,1,0:T(8,128)S(1)}, u32[]{:S(2)}, u32[]{:S(2)}) collective-permute-start(f32[8,2,8,128]{3,2,1,0:T(8,128)S(1)} %get-tuple-element.66), channel_id=1, source_target_pairs={{0,16},{1,17},{2,18},{3,19},{4,20},{5,21},{6,22},{7,23},{8,24},{9,... | collective-permute-start | bytes 196616 | tf_op jit(solution)/shard_map/ppermute | solution.py:24
  8.1 1.3 %collective-permute-start.1 = (f32[8,2,8,128]{3,2,1,0:T(8,128)S(1)}, f32[8,2,8,128]{3,2,1,0:T(8,128)S(1)}, u32[]{:S(2)}, u32[]{:S(2)}) collective-permute-start(f32[8,2,8,128]{3,2,1,0:T(8,128)S(1)} %get-tuple-element.67), channel_id=1, source_target_pairs={{16,0},{17,1},{18,2},{19,3},{20,4},{21,5},{22,6},{23,7},{24,8},{25... | collective-permute-start | bytes 196616 | tf_op jit(solution)/shard_map/ppermute | solution.py:26
  9.4 0.6 %collective-permute-done = f32[8,2,8,128]{3,2,1,0:T(8,128)S(1)} collective-permute-done((f32[8,2,8,128]{3,2,1,0:T(8,128)S(1)}, f32[8,2,8,128]{3,2,1,0:T(8,128)S(1)}, u32[]{:S(2)}, u32[]{:S(2)}) %collective-permute-start) | collective-permute-done | bytes 65568 | tf_op jit(solution)/shard_map/ppermute | solution.py:24
  10.0 4.3 %collective-permute-done.1 = f32[8,2,8,128]{3,2,1,0:T(8,128)S(1)} collective-permute-done((f32[8,2,8,128]{3,2,1,0:T(8,128)S(1)}, f32[8,2,8,128]{3,2,1,0:T(8,128)S(1)}, u32[]{:S(2)}, u32[]{:S(2)}) %collective-permute-start.1) | collective-permute-done | bytes 65568 | tf_op jit(solution)/shard_map/ppermute | solution.py:26
  14.3 1.1 %pad_maximum_fusion.29 = (f32[8,12,2,128]{3,2,1,0:T(2,128)S(1)}, f32[8,12,2,128]{3,2,1,0:T(2,128)S(1)}) fusion(f32[8,2,8,128]{3,2,1,0:T(8,128)S(1)} %collective-permute-done.1, f32[8,2,8,128]{3,2,1,0:T(8,128)S(1)} %collective-permute-done, f32[3,8,8,128]{3,2,1,0:T(8,128)} %param.8, f32[1,8,8,128]{3,2,1,0:T(8,128)S(1)} %fusion.21, ...), kind=kLoop, calls=%fused_computation.137 | loop fusion | flops 245760 | bytes 589824 | tf_op jit(solution)/shard_map/slice | solution.py:21
  15.4 3.5 %collective-permute-start.2 = (f32[8,12,2,128]{3,2,1,0:T(2,128)S(1)}, f32[8,12,2,128]{3,2,1,0:T(2,128)S(1)}, u32[]{:S(2)}, u32[]{:S(2)}) collective-permute-start(f32[8,12,2,128]{3,2,1,0:T(2,128)S(1)} %get-tuple-element.64), channel_id=1, source_target_pairs={{0,4},{4,8},{8,12},{1,5},{5,9},{9,13},{2,6},{6,10},{10,14},{3,7},{... | collective-permute-start | bytes 294920 | tf_op jit(solution)/shard_map/ppermute | solution.py:24
  18.9 1.3 %collective-permute-start.3 = (f32[8,12,2,128]{3,2,1,0:T(2,128)S(1)}, f32[8,12,2,128]{3,2,1,0:T(2,128)S(1)}, u32[]{:S(2)}, u32[]{:S(2)}) collective-permute-start(f32[8,12,2,128]{3,2,1,0:T(2,128)S(1)} %get-tuple-element.65), channel_id=1, source_target_pairs={{4,0},{8,4},{12,8},{5,1},{9,5},{13,9},{6,2},{10,6},{14,10},{7,3},{... | collective-permute-start | bytes 294920 | tf_op jit(solution)/shard_map/ppermute | solution.py:26
  20.2 1.1 %pad_maximum_fusion.36 = (f32[8,12,1,128]{3,2,1,0:T(1,128)S(1)}, f32[8,12,1,128]{3,2,1,0:T(1,128)S(1)}) fusion(f32[8,2,8,128]{3,2,1,0:T(8,128)S(1)} %collective-permute-done.1, f32[8,2,8,128]{3,2,1,0:T(8,128)S(1)} %collective-permute-done, f32[3,8,8,128]{3,2,1,0:T(8,128)} %param.8, f32[1,8,8,128]{3,2,1,0:T(8,128)S(1)} %fusion.21, ...), kind=kLoop, calls=%fused_computation.146 | loop fusion | flops 122880 | bytes 491520 | tf_op jit(solution)/shard_map/slice | solution.py:188
  21.3 0.1 maximum_select_fusion
  21.4 4.0 %collective-permute-done.3 = f32[8,12,2,128]{3,2,1,0:T(2,128)S(1)} collective-permute-done((f32[8,12,2,128]{3,2,1,0:T(2,128)S(1)}, f32[8,12,2,128]{3,2,1,0:T(2,128)S(1)}, u32[]{:S(2)}, u32[]{:S(2)}) %collective-permute-start.3) | collective-permute-done | bytes 98336 | tf_op jit(solution)/shard_map/ppermute | solution.py:26
  25.4 0.1 maximum_select_fusion.1
  25.5 0.1 pad_maximum_fusion.1
  25.8 0.3 fusion.94
  26.1 0.7 %copy.51 = f32[8,12,12,2]{2,0,3,1:T(8,128)S(1)} copy(f32[8,12,12,2]{3,2,1,0:T(8,128)S(1)} %get-tuple-element.56) | data formatting | bytes 18432 | tf_op jit(solution)/shard_map/slice | solution.py:21
  26.8 0.7 %copy.52 = f32[8,12,12,2]{2,0,3,1:T(8,128)S(1)} copy(f32[8,12,12,2]{3,2,1,0:T(8,128)S(1)} %get-tuple-element.57) | data formatting | bytes 18432 | tf_op jit(solution)/shard_map/slice | solution.py:20
  27.5 0.5 %collective-permute-start.4 = (f32[8,12,12,2]{2,0,3,1:T(8,128)S(1)}, f32[8,12,12,2]{2,0,3,1:T(8,128)S(1)}, u32[]{:S(2)}, u32[]{:S(2)}) collective-permute-start(f32[8,12,12,2]{2,0,3,1:T(8,128)S(1)} %copy.51), channel_id=1, source_target_pairs={{0,1},{1,2},{2,3},{3,0},{4,5},{5,6},{6,7},{7,4},{8,9},{9,10},{10,1... | collective-permute-start | bytes 27656 | tf_op jit(solution)/shard_map/ppermute | solution.py:24
  28.0 4.7 %collective-permute-done.4 = f32[8,12,12,2]{2,0,3,1:T(8,128)S(1)} collective-permute-done((f32[8,12,12,2]{2,0,3,1:T(8,128)S(1)}, f32[8,12,12,2]{2,0,3,1:T(8,128)S(1)}, u32[]{:S(2)}, u32[]{:S(2)}) %collective-permute-start.4) | collective-permute-done | bytes 9248 | tf_op jit(solution)/shard_map/ppermute | solution.py:24
  32.7 0.7 %copy.53 = f32[8,12,12,2]{3,2,1,0:T(8,128)S(1)} copy(f32[8,12,12,2]{2,0,3,1:T(8,128)S(1)} %collective-permute-done.4) | data formatting | bytes 18432 | tf_op jit(solution)/shard_map/ppermute | solution.py:24
  33.4 0.7 %copy.54 = f32[8,12,12,2]{3,2,1,0:T(8,128)S(1)} copy(f32[8,12,12,2]{2,0,3,1:T(8,128)S(1)} %collective-permute-done.5) | data formatting | bytes 18432 | tf_op jit(solution)/shard_map/ppermute | solution.py:26
  34.1 0.1 maximum_bitcast_fusion.4
  34.2 0.1 maximum_bitcast_fusion
  34.3 0.7 %pad_maximum_fusion = f32[8,12,12,132]{3,2,1,0:T(8,128)S(1)} fusion(f32[8,12,12,2]{3,2,1,0:T(8,128)S(1)} %copy.54, f32[8,2,12,128]{3,2,1,0:T(8,128)S(1)} %get-tuple-element.59, f32[8,8,12,128]{3,2,1,0:T(8,128)S(1)} %slice.607, f32[8,2,12,128]{3,2,1,0:T(8,128)S(1)} %get-tuple-element.58, f32[8,12,12,2]{3,2,1,0:T(8,128)S(1)} %copy.53), kind=kLoop, calls=%fused_computation | loop fusion | flops 608256 | bytes 1216512 | tf_op jit(solution)/shard_map/concatenate | solution.py:22
  35.0 0.1 slice_bitcast_fusion.6
  35.2 0.1 slice.648
  35.3 0.1 slice.670
  35.7 0.1 slice.623
  35.9 0.1 fusion.89
  36.2 0.6 %add_multiply_fusion.3 = (f32[12,12,132]{2,1,0:T(8,128)S(1)}, f32[12,12,132]{2,1,0:T(8,128)S(1)}, f32[12,12,132]{2,1,0:T(8,128)S(1)}) fusion(f32[12,12,132]{2,1,0:T(8,128)S(1)} %get-tuple-element.55, f32[11,12,132]{2,1,0:T(8,128)S(1)} %get-tuple-element.52, f32[1,12,132]{2,1,0:T(8,128)S(1)} %get-tuple-element.31, f32[11,12,132]{2,1,0:T(8,128)S(1)} %slice.621, ...), kind=kLoop, calls=%fused_computation.68 | loop fusion | flops 1235520 | bytes 1216512 | tf_op jit(solution)/shard_map/mul | solution.py:119
  36.8 0.3 add_multiply_fusion.13
  37.3 0.3 add_multiply_fusion.18
  37.6 0.5 %add_multiply_fusion.8 = (f32[12,12,132]{2,1,0:T(8,128)S(1)}, f32[12,12,132]{2,1,0:T(8,128)S(1)}) fusion(f32[12,12,132]{2,1,0:T(8,128)S(1)} %get-tuple-element.6, f32[11,12,132]{2,1,0:T(8,128)S(1)} %get-tuple-element.49, f32[1,12,132]{2,1,0:T(8,128)S(1)} %get-tuple-element.30, f32[11,12,132]{2,1,0:T(8,128)S(1)} %get-tuple-element.52, ...), kind=kLoop, calls=%fused_computation.73 | loop fusion | flops 1444608 | bytes 1444608 | tf_op jit(solution)/shard_map/mul | solution.py:119
  38.1 0.3 add_multiply_fusion.21
  38.4 0.3 add_multiply_fusion.4
  38.8 0.8 %add_multiply_fusion.2 = (f32[12,12,132]{2,1,0:T(8,128)S(1)}, f32[12,12,132]{2,1,0:T(8,128)S(1)}, f32[12,12,132]{2,1,0:T(8,128)S(1)}) fusion(f32[12,12,132]{2,1,0:T(8,128)S(1)} %get-tuple-element.48, f32[12,11,132]{2,1,0:T(8,128)S(1)} %bitcast.315, f32[12,1,132]{2,1,0:T(1,128)S(1)} %slice.666, f32[12,11,132]{2,1,0:T(8,128)S(1)} %bitcast.288, ...), kind=kLoop, calls=%fused_computation.67 | loop fusion | flops 1235520 | bytes 1216512 | tf_op jit(solution)/shard_map/mul | solution.py:119
  39.6 0.4 add_multiply_fusion.15
  40.0 0.3 add_multiply_fusion.1
  40.4 0.6 %add_multiply_fusion.7 = f32[12,12,132]{2,1,0:T(8,128)S(1)} fusion(f32[12,12,132]{2,1,0:T(8,128)S(1)} %get-tuple-element.17, f32[12,12,132]{2,1,0:T(8,128)S(1)} %get-tuple-element.9, f32[12,12,132]{2,1,0:T(8,128)S(1)} %get-tuple-element.8, f32[12,11,132]{2,1,0:T(8,128)S(1)} %bitcast.328, f32[12,1,132]{2,1,0:T(1,128)S(1)} %slice.699, ...), kind=kLoop, calls=%fused_computation.72 | loop fusion | flops 1273536 | bytes 1368576 | tf_op jit(solution)/shard_map/mul | solution.py:119
  41.1 0.3 maximum_subtract_fusion.1
  41.4 0.3 maximum_subtract_fusion.3
  41.8 0.8 %add_multiply_fusion.5 = (f32[12,12,132]{2,1,0:T(8,128)S(1)}, f32[12,12,132]{2,1,0:T(8,128)S(1)}, f32[12,12,132]{2,1,0:T(8,128)S(1)}, f32[12,12,132]{2,1,0:T(8,1...) fusion(f32[12,12,132]{2,1,0:T(8,128)S(1)} %get-tuple-element.48, f32[12,12,131]{2,1,0:T(8,128)S(1)} %bitcast.318, ...), kind=kLoop, calls=%fused_computation.70 | loop fusion | flops 1235520 | bytes 1444608 | tf_op jit(solution)/shard_map/mul | solution.py:119
  42.6 0.4 add_multiply_fusion.9
  43.0 0.6 %add_multiply_fusion.6 = f32[12,12,132]{2,1,0:T(8,128)S(1)} fusion(f32[12,12,132]{2,1,0:T(8,128)S(1)} %get-tuple-element.17, f32[12,12,132]{2,1,0:T(8,128)S(1)} %get-tuple-element.14, f32[12,12,132]{2,1,0:T(8,128)S(1)} %get-tuple-element.15, f32[12,12,132]{2,1,0:T(8,128)S(1)} %get-tuple-element.12, f32[12,12,132]{2,1,0:T(8,128)S(1)} %get-tuple-element.13, ...), kind=kLoop, calls=%fused_computation.71 | loop fusion | flops 1178496 | bytes 1444608 | tf_op jit(solution)/shard_map/mul | solution.py:119
  43.6 0.4 add_multiply_fusion
  44.1 0.2 fusion.8
  44.5 0.4 fusion.5
  45.0 0.1 slice.747
  45.1 0.1 slice.703
  45.3 0.1 slice.656
  45.4 0.1 slice.688
  45.5 0.1 slice.715
  45.7 0.1 slice.672
  45.8 0.1 slice.730
  46.0 0.1 fusion.74
  46.1 0.2 fusion.79
  46.3 0.6 %pad_maximum_fusion.30 = f32[3,8,8,128]{3,2,1,0:T(8,128)} fusion(f32[1,8,8,128]{3,2,1,0:T(8,128)S(1)} %get-tuple-element.69, f32[1,8,8,128]{3,2,1,0:T(8,128)S(1)} %fusion.74, f32[1,8,8,128]{3,2,1,0:T(8,128)S(1)} %get-tuple-element.68), kind=kLoop, calls=%fused_computation.140 | loop fusion | flops 49152 | bytes 196608 | tf_op jit(solution)/shard_map/stack | solution.py:183
  46.9 0.1 fusion.68
  47.1 0.1 fusion.59
  47.2 0.1 fusion.49
  47.4 0.1 fusion.40
  47.5 0.2 fusion.31
  47.7 0.7 %copy-done.5 = f32[5,8,8,128]{3,2,1,0:T(8,128)} copy-done((f32[5,8,8,128]{3,2,1,0:T(8,128)}, f32[5,8,8,128]{3,2,1,0:T(8,128)S(1)}, u32[]{:S(2)}) %copy-start.5) | copy-done | bytes 163864
  (87 shorter events, 1.6 us)
Async XLA Ops:
  0.6 24.8 %copy-start.4 = (f32[8,8,128]{2,1,0:T(8,128)S(1)}, f32[8,8,128]{2,1,0:T(8,128)}, u32[]{:S(2)}) copy-start(f32[8,8,128]{2,1,0:T(8,128)} %param.5) | copy-start | bytes 98308
  0.6 24.8 %copy-start = (f32[3,8,8,128]{3,2,1,0:T(8,128)S(1)}, f32[3,8,8,128]{3,2,1,0:T(8,128)}, u32[]{:S(2)}) copy-start(f32[3,8,8,128]{3,2,1,0:T(8,128)} %param.8) | copy-start | bytes 294916
  0.7 24.8 %copy-start.1 = (f32[3,8,8,128]{3,2,1,0:T(8,128)S(1)}, f32[3,8,8,128]{3,2,1,0:T(8,128)}, u32[]{:S(2)}) copy-start(f32[3,8,8,128]{3,2,1,0:T(8,128)} %param.6) | copy-start | bytes 294916
  3.2 6.8 %collective-permute-start = (f32[8,2,8,128]{3,2,1,0:T(8,128)S(1)}, f32[8,2,8,128]{3,2,1,0:T(8,128)S(1)}, u32[]{:S(2)}, u32[]{:S(2)}) collective-permute-start(f32[8,2,8,128]{3,2,1,0:T(8,128)S(1)} %get-tuple-element.66), channel_id=1, source_target_pairs={{0,16},{1,17},{2,18},{3,19},{4,20},{5,21},{6,22},{7,23},{8,24},{9,... | collective-permute-start | bytes 196616 | tf_op jit(solution)/shard_map/ppermute | solution.py:24
  8.1 6.2 %collective-permute-start.1 = (f32[8,2,8,128]{3,2,1,0:T(8,128)S(1)}, f32[8,2,8,128]{3,2,1,0:T(8,128)S(1)}, u32[]{:S(2)}, u32[]{:S(2)}) collective-permute-start(f32[8,2,8,128]{3,2,1,0:T(8,128)S(1)} %get-tuple-element.67), channel_id=1, source_target_pairs={{16,0},{17,1},{18,2},{19,3},{20,4},{21,5},{22,6},{23,7},{24,8},{25... | collective-permute-start | bytes 196616 | tf_op jit(solution)/shard_map/ppermute | solution.py:26
  15.4 5.9 %collective-permute-start.2 = (f32[8,12,2,128]{3,2,1,0:T(2,128)S(1)}, f32[8,12,2,128]{3,2,1,0:T(2,128)S(1)}, u32[]{:S(2)}, u32[]{:S(2)}) collective-permute-start(f32[8,12,2,128]{3,2,1,0:T(2,128)S(1)} %get-tuple-element.64), channel_id=1, source_target_pairs={{0,4},{4,8},{8,12},{1,5},{5,9},{9,13},{2,6},{6,10},{10,14},{3,7},{... | collective-permute-start | bytes 294920 | tf_op jit(solution)/shard_map/ppermute | solution.py:24
  18.9 6.5 %collective-permute-start.3 = (f32[8,12,2,128]{3,2,1,0:T(2,128)S(1)}, f32[8,12,2,128]{3,2,1,0:T(2,128)S(1)}, u32[]{:S(2)}, u32[]{:S(2)}) collective-permute-start(f32[8,12,2,128]{3,2,1,0:T(2,128)S(1)} %get-tuple-element.65), channel_id=1, source_target_pairs={{4,0},{8,4},{12,8},{5,1},{9,5},{13,9},{6,2},{10,6},{14,10},{7,3},{... | collective-permute-start | bytes 294920 | tf_op jit(solution)/shard_map/ppermute | solution.py:26
  27.5 5.9 %collective-permute-start.5 = (f32[8,12,12,2]{2,0,3,1:T(8,128)S(1)}, f32[8,12,12,2]{2,0,3,1:T(8,128)S(1)}, u32[]{:S(2)}, u32[]{:S(2)}) collective-permute-start(f32[8,12,12,2]{2,0,3,1:T(8,128)S(1)} %copy.52), channel_id=1, source_target_pairs={{1,0},{2,1},{3,2},{0,3},{5,4},{6,5},{7,6},{4,7},{9,8},{10,9},{11,1... | collective-permute-start | bytes 27656 | tf_op jit(solution)/shard_map/ppermute | solution.py:26
  27.5 5.2 %collective-permute-start.4 = (f32[8,12,12,2]{2,0,3,1:T(8,128)S(1)}, f32[8,12,12,2]{2,0,3,1:T(8,128)S(1)}, u32[]{:S(2)}, u32[]{:S(2)}) collective-permute-start(f32[8,12,12,2]{2,0,3,1:T(8,128)S(1)} %copy.51), channel_id=1, source_target_pairs={{0,1},{1,2},{2,3},{3,0},{4,5},{5,6},{6,7},{7,4},{8,9},{9,10},{10,1... | collective-permute-start | bytes 27656 | tf_op jit(solution)/shard_map/ppermute | solution.py:24
  43.6 1.9 %copy-start.2 = (f32[12,12,132]{2,1,0:T(8,128)}, f32[12,12,132]{2,1,0:T(8,128)S(1)}, u32[]{:S(2)}) copy-start(f32[12,12,132]{2,1,0:T(8,128)S(1)} %add_multiply_fusion.6) | copy-start | bytes 228100
  46.3 1.2 %copy-start.3 = (f32[12,12,132]{2,1,0:T(8,128)S(1)}, f32[12,12,132]{2,1,0:T(8,128)}, u32[]{:S(2)}) copy-start(f32[12,12,132]{2,1,0:T(8,128)} %copy-done.2) | copy-start | bytes 228100
  46.3 1.2 %slice-start = ((f32[12,12,132]{2,1,0:T(8,128)}), f32[12,12,1]{2,1,0:T(8,128)S(1)}, s32[]{:S(2)}) async-start(f32[12,12,132]{2,1,0:T(8,128)} %copy-done.2), calls=%async_computation | async-start | bytes 196608 | tf_op jit(solution)/shard_map/jit(_roll_static)/slice | solution.py:34
  47.7 0.7 %copy-start.5 = (f32[5,8,8,128]{3,2,1,0:T(8,128)}, f32[5,8,8,128]{3,2,1,0:T(8,128)S(1)}, u32[]{:S(2)}) copy-start(f32[5,8,8,128]{3,2,1,0:T(8,128)S(1)} %fusion.31) | copy-start | bytes 491524
where the time goes:
time: 48.8 us; the launch traced here: 48.3 us
  other arithmetic  15.6 us (32%)
  waiting for transfers between devices  13.5 us (28%)
  starting transfers between devices  11.5 us (24%)
  local copies, waits for them, and re-layouts  6.14 us (13%)
  between operations  1.61 us (3%)
    ppermute x3, starting transfers between devices, with_halo(): lax.ppermute(tail, axis, [(i, (i + 1) % count) for i in range(ends)])  8.86 us
    ppermute x3, waiting for transfers between devices, with_halo(): lax.ppermute(head, axis, [((i + 1) % count, i) for i in range(ends)])  8.26 us
    mul x14, other arithmetic, interface_flux(): (fastest * lower_flux - slowest * upper_flux + slowest * fastest * jump)...  6.56 us
    ppermute x3, waiting for transfers between devices, with_halo(): lax.ppermute(tail, axis, [(i, (i + 1) % count) for i in range(ends)])  5.21 us
    ppermute x3, starting transfers between devices, with_halo(): lax.ppermute(head, axis, [((i + 1) % count, i) for i in range(ends)])  2.63 us
    slice x2, other arithmetic, with_halo(): lax.slice_in_dim(cells, cells.shape[dim] - width, cells.shape[dim], axis=...  1.91 us
    slice x47, local copies, waits for them, and re-layouts, shift_up(): return jnp.roll(values, -1, along)  1.25 us
    slice x1, other arithmetic, clamp_dim(): lower_edge = lax.slice_in_dim(extended, 2, 3, axis=dim)  1.11 us
  transfers between devices with their start and end apart: 6, of which 4 were waited for; matrix products, arithmetic and copies ran while one was open for 4% of the time, Pallas kernels for 0%

commit v1 on v0

v1 whole, which is shorter than its diff:
```python
import functools

import jax
import jax.numpy as jnp
from jax import lax
from jax.experimental import pallas as pl
from jax.experimental.pallas import tpu as pltpu
from jax.sharding import PartitionSpec as P

COOL_STEPS = 8
adiabatic = 5.0 / 3.0
courant = 0.08
cool_rate = 0.03
gravity = 1.0

MESH = pl.DeviceIdType.MESH
DIRS = ((0, -1), (0, 1), (-1, 0), (1, 0), (-1, -1), (-1, 1), (1, -1), (1, 1))
FIELDS = 8
FZ, FY, FX = 5, 6, 7
PARTS = 15


def fast_speed(sound, normal_sq, transverse_sq, inv_rho):
    along = normal_sq * inv_rho
    across = transverse_sq * inv_rho
    gap = sound - along - across
    return jnp.sqrt(0.5 * (sound + along + across + jnp.sqrt(gap * gap + 4.0 * sound * across)))


def state_terms(cell, velocity, pressure, magnetic, axis):
    rho, inv_rho, sound, hydro, momenta = cell
    others = [c for c in range(3) if c != axis]
    normal = magnetic[axis]
    normal_sq = normal * normal
    transverse_sq = magnetic[others[0]] * magnetic[others[0]] + magnetic[others[1]] * magnetic[others[1]]
    squared = transverse_sq + normal_sq
    half = 0.5 * squared
    total = pressure + half
    energy = hydro + half
    align = velocity[0] * magnetic[0] + velocity[1] * magnetic[1] + velocity[2] * magnetic[2]
    speed = fast_speed(sound, normal_sq, transverse_sq, inv_rho)
    va = velocity[axis]
    conserved = [rho] + list(momenta) + [energy] + [magnetic[c] for c in others]
    fluxes = [momenta[axis]]
    for c in range(3):
        moment = momenta[c] * va - magnetic[c] * normal
        if c == axis:
            moment = moment + total
        fluxes.append(moment)
    fluxes.append((energy + total) * va - normal * align)
    for c in others:
        fluxes.append(va * magnetic[c] - velocity[c] * normal)
    return va, speed, conserved, fluxes


def cell_terms(rho, velocity, pressure):
    inv_rho = 1.0 / rho
    momenta = [rho * v for v in velocity]
    kinetic = momenta[0] * velocity[0] + momenta[1] * velocity[1] + momenta[2] * velocity[2]
    hydro = pressure * (1.0 / (adiabatic - 1.0)) + 0.5 * kinetic
    return rho, inv_rho, adiabatic * pressure * inv_rho, hydro, momenta


def hll(lower, upper):
    slow = jnp.minimum(jnp.minimum(lower[0] - lower[1], upper[0] - upper[1]), 0.0)
    fast = jnp.maximum(jnp.maximum(lower[0] + lower[1], upper[0] + upper[1]), 0.0)
    inverse = 1.0 / (fast - slow)
    wl = fast * inverse
    wu = -slow * inverse
    wj = slow * wl
    return [
        wl * lower[3][m] + wu * upper[3][m] + wj * (upper[2][m] - lower[2][m]) for m in range(7)
    ]


def kernel(
    sizes, rho_ref, vel_ref, pre_ref, fld_ref, corona_ref, cons_ref, face_ref,
    cooled, sbuf, rbuf, pad, ext, part, res, send_sem, recv_sem,
):
    nz, ny, nx, gz, gy, gx = sizes
    plane = nz * ny
    wide = ny + 3
    iz, iy, ix = lax.axis_index("gz"), lax.axis_index("gy"), lax.axis_index("gx")
    left = lax.rem(ix + gx - 1, gx)
    right = lax.rem(ix + 1, gx)

    has = {-1: {}, 1: {}}
    has_z = {-1: iz > 0, 0: None, 1: iz < gz - 1}
    has_y = {-1: iy > 0, 0: None, 1: iy < gy - 1}

    def exists(dz, dy):
        if dz == 0:
            return has_y[dy]
        if dy == 0:
            return has_z[dz]
        return jnp.logical_and(has_z[dz], has_y[dy])

    barrier = pltpu.get_barrier_semaphore()
    for to in (left, right):
        pl.semaphore_signal(barrier, inc=1, device_id={"gx": to}, device_id_type=MESH)
    for dz, dy in DIRS:
        @pl.when(exists(dz, dy))
        def _():
            pl.semaphore_signal(
                barrier, inc=1, device_id={"gz": iz + dz, "gy": iy + dy}, device_id_type=MESH
            )

    for z in range(nz):
        rows = pl.ds(z * ny, ny)
        rho = rho_ref[rows, :]
        start = pre_ref[rows, :]
        p = start
        for _ in range(COOL_STEPS):
            p = p / (1.0 + cool_rate * jnp.sqrt(rho * p))
        mark = jnp.full(p.shape, corona_ref[iz * nz + z], jnp.int32)
        cooled[rows, :] = jnp.where(mark == 1, p, start)

    sources = (
        [(rho_ref, 0)] + [(vel_ref, c * plane) for c in range(3)] + [(cooled, 0)]
        + [(fld_ref, c * plane) for c in range(3)]
    )

    def y_rows(f, y):
        ref, base = sources[f]
        return ref[pl.ds(base + y, nz, stride=ny), :]

    def z_rows(f, z):
        ref, base = sources[f]
        return ref[pl.ds(base + z * ny, ny), :]

    def one_row(f, z, y):
        ref, base = sources[f]
        return ref[pl.ds(base + z * ny + y, 1), :]

    zf, yf = FIELDS * ny, FIELDS * nz
    for f in range(FIELDS):
        for d, at in ((0, 0), (1, ny - 1)):
            sbuf[d, pl.ds(f * nz, nz), :] = y_rows(f, at)
        for d, at in ((2, 0), (3, nz - 1)):
            sbuf[d, pl.ds(f * ny, ny), :] = z_rows(f, at)
        for d in range(4, 8):
            dz, dy = DIRS[d]
            sbuf[d, pl.ds(f, 1), :] = one_row(f, 0 if dz < 0 else nz - 1, 0 if dy < 0 else ny - 1)
    sbuf[0, pl.ds(yf, nz), :] = y_rows(FY, 1)
    sbuf[2, pl.ds(zf, ny), :] = z_rows(FZ, 1)
    sbuf[5, pl.ds(FIELDS, 1), :] = one_row(FZ, 1, ny - 1)
    sbuf[6, pl.ds(FIELDS, 1), :] = one_row(FY, nz - 1, 1)
    size = (yf + nz, yf, zf + ny, zf, 16, 16, 16, 16)

    for f in range(FIELDS):
        for z in range(nz):
            pad[pl.ds(f * 128 + (z + 1) * wide + 1, ny), :] = z_rows(f, z)

    pl.semaphore_wait(
        barrier,
        2 + sum(exists(dz, dy).astype(jnp.int32) for dz, dy in DIRS),
    )

    def message(d):
        dz, dy = DIRS[d]
        return pltpu.make_async_remote_copy(
            src_ref=sbuf.at[d, pl.ds(0, size[d])],
            dst_ref=rbuf.at[d, pl.ds(0, size[d])],
            send_sem=send_sem.at[d],
            recv_sem=recv_sem.at[d],
            device_id={"gz": iz + dz, "gy": iy + dy},
            device_id_type=MESH,
        )

    for d in (4, 5, 6, 7, 0, 1, 2, 3):
        @pl.when(exists(*DIRS[d]))
        def _():
            message(d).start()

    for d in range(4):
        dz, dy = DIRS[d]
        own = DIRS.index((-dz, -dy))
        step = nz if dz == 0 else ny

        @pl.when(jnp.logical_not(exists(-dz, -dy)))
        def _():
            for f in range(FIELDS):
                rbuf[d, pl.ds(f * step, step), :] = sbuf[own, pl.ds(f * step, step), :]
            if dz + dy < 0:
                f = FY if dz == 0 else FZ
                rbuf[d, pl.ds(FIELDS * step, step), :] = sbuf[own, pl.ds(f * step, step), :]

    for d in range(8):
        dz, dy = DIRS[d]

        @pl.when(exists(-dz, -dy))
        def _():
            message(d).wait_recv()

    for f in range(FIELDS):
        base = f * 128
        pad[pl.ds(base + wide, nz, stride=wide), :] = rbuf[1, pl.ds(f * nz, nz), :]
        pad[pl.ds(base + wide + ny + 1, nz, stride=wide), :] = rbuf[0, pl.ds(f * nz, nz), :]
        pad[pl.ds(base + 1, ny), :] = rbuf[3, pl.ds(f * ny, ny), :]
        pad[pl.ds(base + (nz + 1) * wide + 1, ny), :] = rbuf[2, pl.ds(f * ny, ny), :]
    pad[pl.ds(FY * 128 + wide + ny + 2, nz, stride=wide), :] = rbuf[0, pl.ds(yf, nz), :]
    pad[pl.ds(FZ * 128 + (nz + 2) * wide + 1, ny), :] = rbuf[2, pl.ds(zf, ny), :]

    def spot(z, y):
        return (z + 1) * wide + y + 1

    for d in range(4, 8):
        dz, dy = DIRS[d]
        zg, yg = (nz if dz < 0 else -1), (ny if dy < 0 else -1)
        zc, yc = min(max(zg, 0), nz - 1), min(max(yg, 0), ny - 1)
        both = exists(-dz, -dy)
        extra = {5: (FZ, 1, 0), 6: (FY, 0, 1)}.get(d)

        @pl.when(both)
        def _():
            pad[pl.ds(spot(zg, yg), FIELDS, stride=128), :] = rbuf[d, pl.ds(0, FIELDS), :]
            if extra:
                f, ez, ey = extra
                pad[pl.ds(f * 128 + spot(zg + ez, yg + ey), 1), :] = rbuf[d, pl.ds(FIELDS, 1), :]

        def copy_rows(zs, ys):
            pad[pl.ds(spot(zg, yg), FIELDS, stride=128), :] = pad[
                pl.ds(spot(zs, ys), FIELDS, stride=128), :
            ]

        @pl.when(jnp.logical_not(has_z[-dz]))
        def _():
            copy_rows(zc, yg)
            if extra:
                f, ez, ey = extra
                pad[pl.ds(f * 128 + spot(zg + ez, yg + ey), 1), :] = pad[
                    pl.ds(f * 128 + spot(zc, yg + ey), 1), :
                ]

        @pl.when(jnp.logical_and(has_z[-dz], jnp.logical_not(has_y[-dy])))
        def _():
            copy_rows(zg, yc)
            if extra:
                f, ez, ey = extra
                pad[pl.ds(f * 128 + spot(zg + ez, yg + ey), 1), :] = pad[
                    pl.ds(f * 128 + spot(zg + ez, yc), 1), :
                ]

    for f in range(FIELDS):
        ext[f, pl.ds(8, nx), :] = pad[pl.ds(f * 128, 128), :].T

    to_left = pltpu.make_async_remote_copy(
        src_ref=ext.at[:, pl.ds(8, 8)],
        dst_ref=ext.at[:, pl.ds(8 + nx, 8)],
        send_sem=send_sem.at[8],
        recv_sem=recv_sem.at[8],
        device_id={"gx": left},
        device_id_type=MESH,
    )
    to_right = pltpu.make_async_remote_copy(
        src_ref=ext.at[:, pl.ds(nx, 8)],
        dst_ref=ext.at[:, pl.ds(0, 8)],
        send_sem=send_sem.at[9],
        recv_sem=recv_sem.at[9],
        device_id={"gx": right},
        device_id_type=MESH,
    )
    to_left.start()
    to_right.start()

    lane = lax.broadcasted_iota(jnp.int32, (8, 128), 1)
    slab = iz * nz - 1
    zglobal = jnp.zeros((8, 128), jnp.int32) + slab
    for j in range(1, nz + 3):
        zglobal = zglobal + (lane >= j * wide).astype(jnp.int32)
    height = (2 * zglobal + 1 - nz * gz).astype(jnp.float32) * (1.0 / (nz * gz))
    pull = -gravity * courant * height

    def up(values, axis):
        return pltpu.roll(values, 128 - (wide if axis == 0 else 1), 1)

    def down(values, axis):
        return pltpu.roll(values, wide if axis == 0 else 1, 1)

    def chunk(k):
        r = 7 + 8 * k
        now = [ext[f, pl.ds(r, 8), :] for f in range(FIELDS)]
        below = [ext[f, pl.ds(r - 1, 8), :] for f in range(7)]
        rho, vel, pre, faces = now[0], now[1:4], now[4], now[5:8]
        centre = [
            0.5 * (faces[0] + up(faces[0], 0)),
            0.5 * (faces[1] + up(faces[1], 1)),
            0.5 * (faces[2] + ext[FX, pl.ds(r + 1, 8), :]),
        ]
        cell = cell_terms(rho, vel, pre)
        fluxes = []
        for axis in range(3):
            if axis == 2:
                lrho, lvel, lpre = below[0], below[1:4], below[4]
                lmag = [
                    0.5 * (below[5] + up(below[5], 0)),
                    0.5 * (below[6] + up(below[6], 1)),
                    faces[2],
                ]
            else:
                lrho, lpre = down(rho, axis), down(pre, axis)
                lvel = [down(v, axis) for v in vel]
                lmag = [faces[c] if c == axis else down(centre[c], axis) for c in range(3)]
            umag = [faces[c] if c == axis else centre[c] for c in range(3)]
            lower = state_terms(cell_terms(lrho, lvel, lpre), lvel, lpre, lmag, axis)
            upper = state_terms(cell, vel, pre, umag, axis)
            fluxes.append(hll(lower, upper))
        squared = centre[0] * centre[0] + centre[1] * centre[1] + centre[2] * centre[2]
        base = [rho] + list(cell[4]) + [cell[3] + 0.5 * squared]
        fz, fy, fx = fluxes
        out = pl.ds(8 * k, 8)
        for m in range(5):
            change = up(fz[m], 0) - fz[m] + up(fy[m], 1) - fy[m]
            value = base[m] - courant * change
            if m == 1:
                value = value + rho * pull
            if m == 4:
                value = value + cell[4][0] * pull
            part[m, out, :] = value
            part[5 + m, out, :] = fx[m]
        part[10, out, :] = 0.25 * (fz[5] + down(fz[5], 1) - fy[5] - down(fy[5], 0))
        part[11, out, :] = fx[5] + down(fx[5], 0) - fz[6]
        part[12, out, :] = fz[6]
        part[13, out, :] = fy[6] - fx[6] - down(fx[6], 1)
        part[14, out, :] = fy[6]

    def body(k, carry):
        chunk(k)
        return carry

    count = nx // 8
    lax.fori_loop(1, count, body, 0)
    to_left.wait_recv()
    to_right.wait_recv()
    chunk(0)
    chunk(count)

    def finish(k, carry):
        at = 8 * k
        here, after, before = pl.ds(at + 1, 8), pl.ds(at + 2, 8), pl.ds(at, 8)
        for m in range(5):
            res[m, before, :] = part[m, here, :] - courant * (part[5 + m, after, :] - part[5 + m, here, :])
        ex = part[10, here, :]
        ey = 0.25 * (part[11, here, :] - part[12, before, :])
        ez = 0.25 * (part[13, here, :] + part[14, before, :])
        ey_next = 0.25 * (part[11, after, :] - part[12, here, :])
        ez_next = 0.25 * (part[13, after, :] + part[14, here, :])
        row = pl.ds(at + 8, 8)
        res[7, before, :] = ext[FX, row, :] - courant * ((up(ez, 1) - ez) - (up(ey, 0) - ey))
        res[6, before, :] = ext[FY, row, :] - courant * ((up(ex, 0) - ex) - (ez_next - ez))
        res[5, before, :] = ext[FZ, row, :] - courant * ((ey_next - ey) - (up(ex, 1) - ex))
        return carry

    lax.fori_loop(0, count, finish, 0)
    for m in range(8):
        pad[pl.ds(m * 128, 128), :] = res[m].T
        target, base = (cons_ref, m * plane) if m < 5 else (face_ref, (m - 5) * plane)
        for z in range(nz):
            target[pl.ds(base + z * ny, ny), :] = pad[pl.ds(m * 128 + (z + 1) * wide + 1, ny), :]

    for d in range(8):
        @pl.when(exists(*DIRS[d]))
        def _():
            message(d).wait_send()
    to_left.wait_send()
    to_right.wait_send()


def on_device(sizes, density, velocity, pressure, field, corona):
    nz, ny, nx = density.shape
    gz, gy, gx = sizes
    plane = nz * ny
    vmem = pl.BlockSpec(memory_space=pltpu.VMEM)
    f32 = jnp.float32
    rows = FIELDS * max(nz, ny) + max(nz, ny)
    conserved, faces = pl.pallas_call(
        functools.partial(kernel, (nz, ny, nx, gz, gy, gx)),
        out_shape=(
            jax.ShapeDtypeStruct((5 * plane, nx), f32),
            jax.ShapeDtypeStruct((3 * plane, nx), f32),
        ),
        in_specs=[vmem] * 4 + [pl.BlockSpec(memory_space=pltpu.SMEM)],
        out_specs=(vmem, vmem),
        scratch_shapes=[
            pltpu.VMEM((plane, nx), f32),
            pltpu.VMEM((8, rows, nx), f32),
            pltpu.VMEM((8, rows, nx), f32),
            pltpu.VMEM((FIELDS * 128, nx), f32),
            pltpu.VMEM((FIELDS, nx + 16, 128), f32),
            pltpu.VMEM((PARTS, nx + 8, 128), f32),
            pltpu.VMEM((8, nx, 128), f32),
            pltpu.SemaphoreType.DMA((10,)),
            pltpu.SemaphoreType.DMA((10,)),
        ],
        compiler_params=pltpu.CompilerParams(collective_id=0, has_side_effects=True),
    )(
        density.reshape(plane, nx),
        velocity.reshape(3 * plane, nx),
        pressure.reshape(plane, nx),
        field.reshape(3 * plane, nx),
        corona,
    )
    return conserved.reshape(5, nz, ny, nx), faces.reshape(3, nz, ny, nx)


def solution(mesh):
    sizes = tuple(mesh.shape[axis] for axis in ("gz", "gy", "gx"))
    return jax.shard_map(
        functools.partial(on_device, sizes),
        mesh=mesh,
        in_specs=(
            P("gz", "gy", "gx"),
            P(None, "gz", "gy", "gx"),
            P("gz", "gy", "gx"),
            P(None, "gz", "gy", "gx"),
            P(),
        ),
        out_specs=(P(None, "gz", "gy", "gx"), P(None, "gz", "gy", "gx")),
        check_vma=False,
    )
```

time: 48.8 us -> 18.7 us (0.38)
  Pallas kernels: 0 us -> 15.6 us
  other arithmetic: 15.6 us -> 0 us
  waiting for transfers between devices: 13.5 us -> 0 us
  starting transfers between devices: 11.5 us -> 0 us
  local copies, waits for them, and re-layouts: 6.14 us -> 2.27 us
  between operations: 1.61 us -> 0.65 us
    pallas_call x0 -> x1, Pallas kernels: none -> 15.6 us  [on_device(): pl.pallas_call(functools.partial(kernel, (nz, ny, nx, gz, gy, gx)), out_s...]
    ppermute x6 -> x0, waiting for transfers between devices: 13.5 us -> none  [the longest x3 8.26 us: with_halo(): lax.ppermute(head, axis, [((i + 1) % count, i) for i in range(ends)])]
    ppermute x6 -> x0, starting transfers between devices: 11.5 us -> none  [the longest x3 8.86 us: with_halo(): lax.ppermute(tail, axis, [(i, (i + 1) % count) for i in range(ends)])]
    mul x19 -> x0, other arithmetic: 7.28 us -> none  [the longest x14 6.56 us: interface_flux(): (fastest * lower_flux - slowest * upper_flux + slowest * fastest * jump)...]
    slice x79 -> x0, local copies, waits for them, and re-layouts: 3.94 us -> none  [the longest x47 1.25 us: shift_up(): return jnp.roll(values, -1, along)]
    slice x5 -> x0, other arithmetic: 3.19 us -> none  [the longest x2 1.91 us: with_halo(): lax.slice_in_dim(cells, cells.shape[dim] - width, cells.shape[dim], axis=...]
    unnamed x12 -> x4, local copies, waits for them, and re-layouts: 0.69 us -> 2.27 us
    ppermute x2 -> x0, local copies, waits for them, and re-layouts: 1.39 us -> none  [the longest x1 0.7 us: with_halo(): lax.ppermute(head, axis, [((i + 1) % count, i) for i in range(ends)])]
  transfers between devices with their start and end apart: 6 -> 0, of which waited for: 4 -> 0; matrix products, arithmetic and copies ran while one was open for 4% -> 0% of each run, Pallas kernels for 0% -> 0%
where the time goes in v1:
time: 18.7 us; the launch traced here: 18.5 us
  Pallas kernels  15.6 us (83%)
  local copies, waits for them, and re-layouts  2.27 us (12%)
  between operations  0.65 us (3%)
    pallas_call x1, Pallas kernels, on_device(): pl.pallas_call(functools.partial(kernel, (nz, ny, nx, gz, gy, gx)), out_s...  15.6 us
    unnamed x4, local copies, waits for them, and re-layouts  2.27 us

profile of v1, /device:TPU:0, one launch (start us, length us, event | category | flops | bytes accessed | tf_op | source)
XLA Modules:
  0.0 18.5 jit_solution(7455560946153518541)
XLA Ops:
  0.6 15.6 %shard_map.68 = (f32[320,128]{1,0:T(8,128)}, f32[192,128]{1,0:T(8,128)}) custom-call(f32[64,128]{1,0:T(8,128)} %bitcast.10, f32[192,128]{1,0:T(8,128)} %bitcast.8, f32[64,128]{1,0:T(8,128)} %bitcast.11, f32[192,128]{1,0:T(8,128)} %bitcast.9, s32[16]{0:T(128)} %corona_ref.1), custom_call_target="tpu_custom_call" | custom-call | tf_op jit(solution)/shard_map/pallas_call | solution.py:376
  16.3 0.0 copy-start
  16.3 1.6 %copy.9 = f32[5,8,8,128]{3,2,1,0:T(8,128)} copy(f32[5,8,8,128]{3,2,1,0:T(8,128)} %bitcast.6) | data formatting | bytes 327680
  17.9 0.0 copy-done
  17.9 0.6 %copy.10 = f32[3,8,8,128]{3,2,1,0:T(8,128)} copy(f32[3,8,8,128]{3,2,1,0:T(8,128)S(1)} %bitcast.7) | data formatting | bytes 196608
Async XLA Ops:
  16.3 1.6 %copy-start = (f32[192,128]{1,0:T(8,128)S(1)}, f32[192,128]{1,0:T(8,128)}, u32[]{:S(2)}) copy-start(f32[192,128]{1,0:T(8,128)} %get-tuple-element.5) | copy-start | bytes 294916

commit v2 on v1

--- a/solution.py
+++ b/solution.py
@@ -74,8 +74,8 @@
 
 
 def kernel(
-    sizes, rho_ref, vel_ref, pre_ref, fld_ref, corona_ref, cons_ref, face_ref,
-    cooled, sbuf, rbuf, pad, ext, part, res, send_sem, recv_sem,
+    sizes, rho_hbm, vel_hbm, pre_hbm, fld_hbm, corona_hbm, res,
+    stack, raw, marks, sbuf, rbuf, pad, ext, part, load_sem, send_sem, recv_sem,
 ):
     nz, ny, nx, gz, gy, gx = sizes
     plane = nz * ny
@@ -84,7 +84,6 @@
     left = lax.rem(ix + gx - 1, gx)
     right = lax.rem(ix + 1, gx)
 
-    has = {-1: {}, 1: {}}
     has_z = {-1: iz > 0, 0: None, 1: iz < gz - 1}
     has_y = {-1: iy > 0, 0: None, 1: iy < gy - 1}
 
@@ -95,6 +94,19 @@
             return has_z[dz]
         return jnp.logical_and(has_z[dz], has_y[dy])
 
+    loads = [
+        pltpu.make_async_copy(src, dst, load_sem.at[i])
+        for i, (src, dst) in enumerate((
+            (rho_hbm, stack.at[pl.ds(0, plane)]),
+            (pre_hbm, raw),
+            (corona_hbm, marks),
+            (fld_hbm, stack.at[pl.ds(FZ * plane, 3 * plane)]),
+            (vel_hbm, stack.at[pl.ds(plane, 3 * plane)]),
+        ))
+    ]
+    for load in loads:
+        load.start()
+
     barrier = pltpu.get_barrier_semaphore()
     for to in (left, right):
         pl.semaphore_signal(barrier, inc=1, device_id={"gx": to}, device_id_type=MESH)
@@ -105,32 +117,29 @@
                 barrier, inc=1, device_id={"gz": iz + dz, "gy": iy + dy}, device_id_type=MESH
             )
 
+    for load in loads[:3]:
+        load.wait()
     for z in range(nz):
         rows = pl.ds(z * ny, ny)
-        rho = rho_ref[rows, :]
-        start = pre_ref[rows, :]
+        rho = stack[rows, :]
+        start = raw[rows, :]
         p = start
         for _ in range(COOL_STEPS):
             p = p / (1.0 + cool_rate * jnp.sqrt(rho * p))
-        mark = jnp.full(p.shape, corona_ref[iz * nz + z], jnp.int32)
-        cooled[rows, :] = jnp.where(mark == 1, p, start)
-
-    sources = (
-        [(rho_ref, 0)] + [(vel_ref, c * plane) for c in range(3)] + [(cooled, 0)]
-        + [(fld_ref, c * plane) for c in range(3)]
-    )
+        mark = jnp.full(p.shape, marks[iz * nz + z], jnp.int32)
+        stack[pl.ds(4 * plane + z * ny, ny), :] = jnp.where(mark == 1, p, start)
+
+    for load in loads[3:]:
+        load.wait()
 
     def y_rows(f, y):
-        ref, base = sources[f]
-        return ref[pl.ds(base + y, nz, stride=ny), :]
+        return stack[pl.ds(f * plane + y, nz, stride=ny), :]
 
     def z_rows(f, z):
-        ref, base = sources[f]
-        return ref[pl.ds(base + z * ny, ny), :]
+        return stack[pl.ds(f * plane + z * ny, ny), :]
 
     def one_row(f, z, y):
-        ref, base = sources[f]
-        return ref[pl.ds(base + z * ny + y, 1), :]
+        return stack[pl.ds(f * plane + z * ny + y, 1), :]
 
     zf, yf = FIELDS * ny, FIELDS * nz
     for f in range(FIELDS):
@@ -352,54 +361,87 @@
         return carry
 
     lax.fori_loop(0, count, finish, 0)
-    for m in range(8):
-        pad[pl.ds(m * 128, 128), :] = res[m].T
-        target, base = (cons_ref, m * plane) if m < 5 else (face_ref, (m - 5) * plane)
-        for z in range(nz):
-            target[pl.ds(base + z * ny, ny), :] = pad[pl.ds(m * 128 + (z + 1) * wide + 1, ny), :]
-
     for d in range(8):
         @pl.when(exists(*DIRS[d]))
         def _():
             message(d).wait_send()
     to_left.wait_send()
     to_right.wait_send()
+
+
+def unpack_kernel(sizes, res, cons_ref, face_ref, turned, out, sem):
+    nz, ny = sizes
+    plane, wide = nz * ny, ny + 3
+    copies = []
+    for m in range(FIELDS):
+        turned[m] = res[m].T
+        for z in range(nz):
+            out[pl.ds(m * plane + z * ny, ny), :] = turned[m, pl.ds((z + 1) * wide + 1, ny), :]
+        target, base = (cons_ref, m * plane) if m < 5 else (face_ref, (m - 5) * plane)
+        copies.append(pltpu.make_async_copy(
+            out.at[pl.ds(m * plane, plane)], target.at[pl.ds(base, plane)], sem.at[m]
+        ))
+        copies[-1].start()
+    for copy in copies:
+        copy.wait()
 
 
 def on_device(sizes, density, velocity, pressure, field, corona):
     nz, ny, nx = density.shape
     gz, gy, gx = sizes
     plane = nz * ny
+    hbm = pl.BlockSpec(memory_space=pltpu.HBM)
     vmem = pl.BlockSpec(memory_space=pltpu.VMEM)
     f32 = jnp.float32
     rows = FIELDS * max(nz, ny) + max(nz, ny)
-    conserved, faces = pl.pallas_call(
+    result = pl.pallas_call(
         functools.partial(kernel, (nz, ny, nx, gz, gy, gx)),
-        out_shape=(
-            jax.ShapeDtypeStruct((5 * plane, nx), f32),
-            jax.ShapeDtypeStruct((3 * plane, nx), f32),
-        ),
-        in_specs=[vmem] * 4 + [pl.BlockSpec(memory_space=pltpu.SMEM)],
-        out_specs=(vmem, vmem),
+        out_shape=pltpu.VMEM((FIELDS, nx, 128), f32),
+        in_specs=[hbm] * 5,
+        out_specs=vmem,
         scratch_shapes=[
+            pltpu.VMEM((FIELDS * plane, nx), f32),
             pltpu.VMEM((plane, nx), f32),
+            pltpu.SMEM(corona.shape, jnp.int32),
             pltpu.VMEM((8, rows, nx), f32),
             pltpu.VMEM((8, rows, nx), f32),
             pltpu.VMEM((FIELDS * 128, nx), f32),
             pltpu.VMEM((FIELDS, nx + 16, 128), f32),
             pltpu.VMEM((PARTS, nx + 8, 128), f32),
-            pltpu.VMEM((8, nx, 128), f32),
+            pltpu.SemaphoreType.DMA((5,)),
             pltpu.SemaphoreType.DMA((10,)),
             pltpu.SemaphoreType.DMA((10,)),
         ],
-        compiler_params=pltpu.CompilerParams(collective_id=0, has_side_effects=True),
+        compiler_params=pltpu.CompilerParams(
+            collective_id=0, has_side_effects=True, vmem_limit_bytes=16 << 20
+        ),
     )(
-        density.reshape(plane, nx),
-        velocity.reshape(3 * plane, nx),
-        pressure.reshape(plane, nx),
-        field.reshape(3 * plane, nx),
-        corona,
+        *(
+            pltpu.with_memory_space_constraint(x, pltpu.HBM)
+            for x in (
+                density.reshape(plane, nx),
+                velocity.reshape(3 * plane, nx),
+                pressure.reshape(plane, nx),
+                field.reshape(3 * plane, nx),
+                corona,
+            )
+        )
     )
+    conserved, faces = pl.pallas_call(
+        functools.partial(unpack_kernel, (nz, ny)),
+        out_shape=(
+            jax.ShapeDtypeStruct((5 * plane, nx), f32),
+            jax.ShapeDtypeStruct((3 * plane, nx), f32),
+        ),
+        in_specs=[vmem],
+        out_specs=(hbm, hbm),
+        scratch_shapes=[
+            pltpu.VMEM((FIELDS, 128, nx), f32),
+            pltpu.VMEM((FIELDS * plane, nx), f32),
+            pltpu.SemaphoreType.DMA((FIELDS,)),
+        ],
+        compiler_params=pltpu.CompilerParams(vmem_limit_bytes=16 << 20),
+    )(result)
     return conserved.reshape(5, nz, ny, nx), faces.reshape(3, nz, ny, nx)
 
 

time: 18.7 us -> 15.5 us (0.83)
  local copies, waits for them, and re-layouts: 2.27 us -> 0 us
  Pallas kernels: 15.6 us -> 14.7 us
    unnamed x4 -> x0, local copies, waits for them, and re-layouts: 2.27 us -> none
    pallas_call x1, Pallas kernels: 15.6 us -> 13.8 us  [on_device(): pl.pallas_call(functools.partial(kernel, (nz, ny, nx, gz, gy, gx)), out_s...]
    pallas_call x0 -> x1, Pallas kernels: none -> 0.93 us  [on_device(): pl.pallas_call(functools.partial(unpack_kernel, (nz, ny)), out_shape=(jax...]
where the time goes in v2:
time: 15.5 us; the launch traced here: 15.3 us
  Pallas kernels  14.7 us (95%)
  between operations  0.64 us (4%)
    pallas_call x1, Pallas kernels, on_device(): pl.pallas_call(functools.partial(kernel, (nz, ny, nx, gz, gy, gx)), out_s...  13.8 us
    pallas_call x1, Pallas kernels, on_device(): pl.pallas_call(functools.partial(unpack_kernel, (nz, ny)), out_shape=(jax...  0.93 us

profile of v2, /device:TPU:0, one launch (start us, length us, event | category | flops | bytes accessed | tf_op | source)
XLA Modules:
  0.0 15.3 jit_solution(7035825647076324592)
XLA Ops:
  0.6 13.8 %shard_map.68.res = f32[8,128,128]{2,1,0:T(8,128)S(1)} custom-call(f32[64,128]{1,0:T(8,128)} %bitcast.8, f32[192,128]{1,0:T(8,128)} %bitcast.6, f32[64,128]{1,0:T(8,128)} %bitcast.9, f32[192,128]{1,0:T(8,128)} %bitcast.7, s32[16]{0:T(128)} %corona_hbm.1), custom_call_target="tpu_custom_call" | custom-call | tf_op jit(solution)/shard_map/pallas_call | solution.py:397
  14.4 0.9 %shard_map.69 = (f32[320,128]{1,0:T(8,128)}, f32[192,128]{1,0:T(8,128)}) custom-call(f32[8,128,128]{2,1,0:T(8,128)S(1)} %shard_map.68.res), custom_call_target="tpu_custom_call" | custom-call | tf_op jit(solution)/shard_map/pallas_call | solution.py:430

commit v3 on v2

--- a/solution.py
+++ b/solution.py
@@ -18,17 +18,22 @@
 FIELDS = 8
 FZ, FY, FX = 5, 6, 7
 PARTS = 15
-
-
-def fast_speed(sound, normal_sq, transverse_sq, inv_rho):
-    along = normal_sq * inv_rho
-    across = transverse_sq * inv_rho
-    gap = sound - along - across
-    return jnp.sqrt(0.5 * (sound + along + across + jnp.sqrt(gap * gap + 4.0 * sound * across)))
+TINY = 1e-36
+
+
+def root(values):
+    return values * lax.rsqrt(values)
+
+
+def fast_speed(half_sound, squared, transverse_sq, half_inverse):
+    both = squared * half_inverse
+    gap = half_sound - both
+    inner = gap * gap + (4.0 * half_sound) * (transverse_sq * half_inverse)
+    return root(half_sound + both + root(jnp.maximum(inner, TINY)))
 
 
 def state_terms(cell, velocity, pressure, magnetic, axis):
-    rho, inv_rho, sound, hydro, momenta = cell
+    rho, half_inverse, half_sound, hydro, momenta = cell
     others = [c for c in range(3) if c != axis]
     normal = magnetic[axis]
     normal_sq = normal * normal
@@ -38,7 +43,7 @@
     total = pressure + half
     energy = hydro + half
     align = velocity[0] * magnetic[0] + velocity[1] * magnetic[1] + velocity[2] * magnetic[2]
-    speed = fast_speed(sound, normal_sq, transverse_sq, inv_rho)
+    speed = fast_speed(half_sound, squared, transverse_sq, half_inverse)
     va = velocity[axis]
     conserved = [rho] + list(momenta) + [energy] + [magnetic[c] for c in others]
     fluxes = [momenta[axis]]
@@ -54,11 +59,11 @@
 
 
 def cell_terms(rho, velocity, pressure):
-    inv_rho = 1.0 / rho
+    half_inverse = 0.5 / rho
     momenta = [rho * v for v in velocity]
     kinetic = momenta[0] * velocity[0] + momenta[1] * velocity[1] + momenta[2] * velocity[2]
     hydro = pressure * (1.0 / (adiabatic - 1.0)) + 0.5 * kinetic
-    return rho, inv_rho, adiabatic * pressure * inv_rho, hydro, momenta
+    return rho, half_inverse, adiabatic * pressure * half_inverse, hydro, momenta
 
 
 def hll(lower, upper):
@@ -75,11 +80,12 @@
 
 def kernel(
     sizes, rho_hbm, vel_hbm, pre_hbm, fld_hbm, corona_hbm, res,
-    stack, raw, marks, sbuf, rbuf, pad, ext, part, load_sem, send_sem, recv_sem,
+    stack, raw, marks, sbuf, rbuf, pad, ext, xsend, xrecv, part, load_sem, send_sem, recv_sem, ready,
 ):
     nz, ny, nx, gz, gy, gx = sizes
     plane = nz * ny
     wide = ny + 3
+    tall = nx + 16
     iz, iy, ix = lax.axis_index("gz"), lax.axis_index("gy"), lax.axis_index("gx")
     left = lax.rem(ix + gx - 1, gx)
     right = lax.rem(ix + 1, gx)
@@ -110,7 +116,7 @@
     barrier = pltpu.get_barrier_semaphore()
     for to in (left, right):
         pl.semaphore_signal(barrier, inc=1, device_id={"gx": to}, device_id_type=MESH)
-    for dz, dy in DIRS:
+    for dz, dy in DIRS[:4]:
         @pl.when(exists(dz, dy))
         def _():
             pl.semaphore_signal(
@@ -160,10 +166,28 @@
         for z in range(nz):
             pad[pl.ds(f * 128 + (z + 1) * wide + 1, ny), :] = z_rows(f, z)
 
+    for d in range(4):
+        dz, dy = DIRS[d]
+        own = DIRS.index((-dz, -dy))
+        step = nz if dz == 0 else ny
+
+        @pl.when(jnp.logical_not(exists(-dz, -dy)))
+        def _():
+            for f in range(FIELDS):
+                rbuf[d, pl.ds(f * step, step), :] = sbuf[own, pl.ds(f * step, step), :]
+            if dz + dy < 0:
+                f = FY if dz == 0 else FZ
+                rbuf[d, pl.ds(FIELDS * step, step), :] = sbuf[own, pl.ds(f * step, step), :]
+
     pl.semaphore_wait(
         barrier,
-        2 + sum(exists(dz, dy).astype(jnp.int32) for dz, dy in DIRS),
+        2 + sum(exists(dz, dy).astype(jnp.int32) for dz, dy in DIRS[:4]),
     )
+
+    for dz in (-1, 1):
+        @pl.when(has_z[dz])
+        def _():
+            pl.semaphore_signal(ready, inc=1, device_id={"gz": iz + dz}, device_id_type=MESH)
 
     def message(d):
         dz, dy = DIRS[d]
@@ -176,23 +200,13 @@
             device_id_type=MESH,
         )
 
-    for d in (4, 5, 6, 7, 0, 1, 2, 3):
+    for d in range(8):
+        if d == 4:
+            pl.semaphore_wait(ready, has_z[-1].astype(jnp.int32) + has_z[1].astype(jnp.int32))
+
         @pl.when(exists(*DIRS[d]))
         def _():
             message(d).start()
-
-    for d in range(4):
-        dz, dy = DIRS[d]
-        own = DIRS.index((-dz, -dy))
-        step = nz if dz == 0 else ny
-
-        @pl.when(jnp.logical_not(exists(-dz, -dy)))
-        def _():
-            for f in range(FIELDS):
-                rbuf[d, pl.ds(f * step, step), :] = sbuf[own, pl.ds(f * step, step), :]
-            if dz + dy < 0:
-                f = FY if dz == 0 else FZ
-                rbuf[d, pl.ds(FIELDS * step, step), :] = sbuf[own, pl.ds(f * step, step), :]
 
     for d in range(8):
         dz, dy = DIRS[d]
@@ -251,27 +265,27 @@
                 ]
 
     for f in range(FIELDS):
-        ext[f, pl.ds(8, nx), :] = pad[pl.ds(f * 128, 128), :].T
+        ext[pl.ds(f * tall + 8, nx), :] = pad[pl.ds(f * 128, 128), :].T
+    xsend[pl.ds(0, FIELDS), :] = ext[pl.ds(8, FIELDS, stride=tall), :]
+    xsend[pl.ds(FIELDS, 1), :] = ext[pl.ds(FX * tall + 9, 1), :]
+    xsend[pl.ds(16, FIELDS), :] = ext[pl.ds(7 + nx, FIELDS, stride=tall), :]
 
     to_left = pltpu.make_async_remote_copy(
-        src_ref=ext.at[:, pl.ds(8, 8)],
-        dst_ref=ext.at[:, pl.ds(8 + nx, 8)],
+        src_ref=xsend.at[pl.ds(0, 16)],
+        dst_ref=xrecv.at[pl.ds(0, 16)],
         send_sem=send_sem.at[8],
         recv_sem=recv_sem.at[8],
         device_id={"gx": left},
         device_id_type=MESH,
     )
     to_right = pltpu.make_async_remote_copy(
-        src_ref=ext.at[:, pl.ds(nx, 8)],
-        dst_ref=ext.at[:, pl.ds(0, 8)],
+        src_ref=xsend.at[pl.ds(16, 8)],
+        dst_ref=xrecv.at[pl.ds(16, 8)],
         send_sem=send_sem.at[9],
         recv_sem=recv_sem.at[9],
         device_id={"gx": right},
         device_id_type=MESH,
     )
-    to_left.start()
-    to_right.start()
-
     lane = lax.broadcasted_iota(jnp.int32, (8, 128), 1)
     slab = iz * nz - 1
     zglobal = jnp.zeros((8, 128), jnp.int32) + slab
@@ -279,6 +293,8 @@
         zglobal = zglobal + (lane >= j * wide).astype(jnp.int32)
     height = (2 * zglobal + 1 - nz * gz).astype(jnp.float32) * (1.0 / (nz * gz))
     pull = -gravity * courant * height
+    to_left.start()
+    to_right.start()
 
     def up(values, axis):
         return pltpu.roll(values, 128 - (wide if axis == 0 else 1), 1)
@@ -288,19 +304,20 @@
 
     def chunk(k):
         r = 7 + 8 * k
-        now = [ext[f, pl.ds(r, 8), :] for f in range(FIELDS)]
-        below = [ext[f, pl.ds(r - 1, 8), :] for f in range(7)]
+        now = [ext[pl.ds(f * tall + r, 8), :] for f in range(FIELDS)]
+        below = [ext[pl.ds(f * tall + r - 1, 8), :] for f in range(7)]
         rho, vel, pre, faces = now[0], now[1:4], now[4], now[5:8]
         centre = [
             0.5 * (faces[0] + up(faces[0], 0)),
             0.5 * (faces[1] + up(faces[1], 1)),
-            0.5 * (faces[2] + ext[FX, pl.ds(r + 1, 8), :]),
+            0.5 * (faces[2] + ext[pl.ds(FX * tall + r + 1, 8), :]),
         ]
         cell = cell_terms(rho, vel, pre)
         fluxes = []
         for axis in range(3):
             if axis == 2:
                 lrho, lvel, lpre = below[0], below[1:4], below[4]
+                lcell = cell_terms(lrho, lvel, lpre)
                 lmag = [
                     0.5 * (below[5] + up(below[5], 0)),
                     0.5 * (below[6] + up(below[6], 1)),
@@ -309,9 +326,13 @@
             else:
                 lrho, lpre = down(rho, axis), down(pre, axis)
                 lvel = [down(v, axis) for v in vel]
+                lcell = (
+                    lrho, down(cell[1], axis), down(cell[2], axis), down(cell[3], axis),
+                    [lrho * v for v in lvel],
+                )
                 lmag = [faces[c] if c == axis else down(centre[c], axis) for c in range(3)]
             umag = [faces[c] if c == axis else centre[c] for c in range(3)]
-            lower = state_terms(cell_terms(lrho, lvel, lpre), lvel, lpre, lmag, axis)
+            lower = state_terms(lcell, lvel, lpre, lmag, axis)
             upper = state_terms(cell, vel, pre, umag, axis)
             fluxes.append(hll(lower, upper))
         squared = centre[0] * centre[0] + centre[1] * centre[1] + centre[2] * centre[2]
@@ -333,18 +354,18 @@
         part[13, out, :] = fy[6] - fx[6] - down(fx[6], 1)
         part[14, out, :] = fy[6]
 
-    def body(k, carry):
+    count = nx // 8
+    for k in range(1, count):
         chunk(k)
-        return carry
-
-    count = nx // 8
-    lax.fori_loop(1, count, body, 0)
     to_left.wait_recv()
     to_right.wait_recv()
+    ext[pl.ds(8 + nx, FIELDS, stride=tall), :] = xrecv[pl.ds(0, FIELDS), :]
+    ext[pl.ds(FX * tall + 9 + nx, 1), :] = xrecv[pl.ds(FIELDS, 1), :]
+    ext[pl.ds(7, FIELDS, stride=tall), :] = xrecv[pl.ds(16, FIELDS), :]
     chunk(0)
     chunk(count)
 
-    def finish(k, carry):
+    def finish(k):
         at = 8 * k
         here, after, before = pl.ds(at + 1, 8), pl.ds(at + 2, 8), pl.ds(at, 8)
         for m in range(5):
@@ -354,13 +375,12 @@
         ez = 0.25 * (part[13, here, :] + part[14, before, :])
         ey_next = 0.25 * (part[11, after, :] - part[12, here, :])
         ez_next = 0.25 * (part[13, after, :] + part[14, here, :])
-        row = pl.ds(at + 8, 8)
-        res[7, before, :] = ext[FX, row, :] - courant * ((up(ez, 1) - ez) - (up(ey, 0) - ey))
-        res[6, before, :] = ext[FY, row, :] - courant * ((up(ex, 0) - ex) - (ez_next - ez))
-        res[5, before, :] = ext[FZ, row, :] - courant * ((ey_next - ey) - (up(ex, 1) - ex))
-        return carry
-
-    lax.fori_loop(0, count, finish, 0)
+        res[7, before, :] = ext[pl.ds(FX * tall + at + 8, 8), :] - courant * ((up(ez, 1) - ez) - (up(ey, 0) - ey))
+        res[6, before, :] = ext[pl.ds(FY * tall + at + 8, 8), :] - courant * ((up(ex, 0) - ex) - (ez_next - ez))
+        res[5, before, :] = ext[pl.ds(FZ * tall + at + 8, 8), :] - courant * ((ey_next - ey) - (up(ex, 1) - ex))
+
+    for k in range(count):
+        finish(k)
     for d in range(8):
         @pl.when(exists(*DIRS[d]))
         def _():
@@ -406,11 +426,14 @@
             pltpu.VMEM((8, rows, nx), f32),
             pltpu.VMEM((8, rows, nx), f32),
             pltpu.VMEM((FIELDS * 128, nx), f32),
-            pltpu.VMEM((FIELDS, nx + 16, 128), f32),
+            pltpu.VMEM((FIELDS * (nx + 16), 128), f32),
+            pltpu.VMEM((24, 128), f32),
+            pltpu.VMEM((24, 128), f32),
             pltpu.VMEM((PARTS, nx + 8, 128), f32),
             pltpu.SemaphoreType.DMA((5,)),
             pltpu.SemaphoreType.DMA((10,)),
             pltpu.SemaphoreType.DMA((10,)),
+            pltpu.SemaphoreType.REGULAR,
         ],
         compiler_params=pltpu.CompilerParams(
             collective_id=0, has_side_effects=True, vmem_limit_bytes=16 << 20

time: 15.5 us -> 13 us (0.84)
  Pallas kernels: 14.7 us -> 12.2 us
    pallas_call x1, Pallas kernels: 13.8 us -> 11.3 us  [on_device(): pl.pallas_call(functools.partial(kernel, (nz, ny, nx, gz, gy, gx)), out_s...]
where the time goes in v3:
time: 13 us; the launch traced here: 12.8 us
  Pallas kernels  12.2 us (94%)
  between operations  0.64 us (5%)
    pallas_call x1, Pallas kernels, on_device(): pl.pallas_call(functools.partial(kernel, (nz, ny, nx, gz, gy, gx)), out_s...  11.3 us
    pallas_call x1, Pallas kernels, on_device(): pl.pallas_call(functools.partial(unpack_kernel, (nz, ny)), out_shape=(jax...  0.93 us

profile of v3, /device:TPU:0, one launch (start us, length us, event | category | flops | bytes accessed | tf_op | source)
XLA Modules:
  0.0 12.8 jit_solution(13684840433128793849)
XLA Ops:
  0.6 11.3 %shard_map.68.res = f32[8,128,128]{2,1,0:T(8,128)S(1)} custom-call(f32[64,128]{1,0:T(8,128)} %bitcast.8, f32[192,128]{1,0:T(8,128)} %bitcast.6, f32[64,128]{1,0:T(8,128)} %bitcast.9, f32[192,128]{1,0:T(8,128)} %bitcast.7, s32[16]{0:T(128)} %corona_hbm.1), custom_call_target="tpu_custom_call" | custom-call | tf_op jit(solution)/shard_map/pallas_call | solution.py:417
  11.9 0.9 %shard_map.69 = (f32[320,128]{1,0:T(8,128)}, f32[192,128]{1,0:T(8,128)}) custom-call(f32[8,128,128]{2,1,0:T(8,128)S(1)} %shard_map.68.res), custom_call_target="tpu_custom_call" | custom-call | tf_op jit(solution)/shard_map/pallas_call | solution.py:453

commit v4 on v3

--- a/solution.py
+++ b/solution.py
@@ -25,8 +25,8 @@
     return values * lax.rsqrt(values)
 
 
-def fast_speed(half_sound, squared, transverse_sq, half_inverse):
-    both = squared * half_inverse
+def fast_speed(half_sound, half_squared, transverse_sq, half_inverse):
+    both = half_squared * (2.0 * half_inverse)
     gap = half_sound - both
     inner = gap * gap + (4.0 * half_sound) * (transverse_sq * half_inverse)
     return root(half_sound + both + root(jnp.maximum(inner, TINY)))
@@ -34,28 +34,19 @@
 
 def state_terms(cell, velocity, pressure, magnetic, axis):
     rho, half_inverse, half_sound, hydro, momenta = cell
-    others = [c for c in range(3) if c != axis]
+    one, two = [c for c in range(3) if c != axis]
     normal = magnetic[axis]
     normal_sq = normal * normal
-    transverse_sq = magnetic[others[0]] * magnetic[others[0]] + magnetic[others[1]] * magnetic[others[1]]
-    squared = transverse_sq + normal_sq
-    half = 0.5 * squared
-    total = pressure + half
+    transverse_sq = magnetic[one] * magnetic[one] + magnetic[two] * magnetic[two]
+    half = 0.5 * (transverse_sq + normal_sq)
     energy = hydro + half
-    align = velocity[0] * magnetic[0] + velocity[1] * magnetic[1] + velocity[2] * magnetic[2]
-    speed = fast_speed(half_sound, squared, transverse_sq, half_inverse)
+    tension = pressure + half - normal_sq
+    align = velocity[one] * magnetic[one] + velocity[two] * magnetic[two]
+    speed = fast_speed(half_sound, half, transverse_sq, half_inverse)
     va = velocity[axis]
-    conserved = [rho] + list(momenta) + [energy] + [magnetic[c] for c in others]
-    fluxes = [momenta[axis]]
-    for c in range(3):
-        moment = momenta[c] * va - magnetic[c] * normal
-        if c == axis:
-            moment = moment + total
-        fluxes.append(moment)
-    fluxes.append((energy + total) * va - normal * align)
-    for c in others:
-        fluxes.append(va * magnetic[c] - velocity[c] * normal)
-    return va, speed, conserved, fluxes
+    conserved = [rho] + list(momenta) + [energy]
+    work = tension * va - normal * align
+    return va, speed, conserved, tension, work, velocity, magnetic
 
 
 def cell_terms(rho, velocity, pressure):
@@ -66,21 +57,42 @@
     return rho, half_inverse, adiabatic * pressure * half_inverse, hydro, momenta
 
 
-def hll(lower, upper):
-    slow = jnp.minimum(jnp.minimum(lower[0] - lower[1], upper[0] - upper[1]), 0.0)
-    fast = jnp.maximum(jnp.maximum(lower[0] + lower[1], upper[0] + upper[1]), 0.0)
+def hll(lower, upper, axis):
+    low, high = lower[0] - lower[1], lower[0] + lower[1]
+    slow = jnp.minimum(jnp.minimum(low, upper[0] - upper[1]), 0.0)
+    fast = jnp.maximum(jnp.maximum(high, upper[0] + upper[1]), 0.0)
     inverse = 1.0 / (fast - slow)
     wl = fast * inverse
     wu = -slow * inverse
     wj = slow * wl
-    return [
-        wl * lower[3][m] + wu * upper[3][m] + wj * (upper[2][m] - lower[2][m]) for m in range(7)
-    ]
+    al = wl * lower[0] - wj
+    au = wu * upper[0] + wj
+    normal = upper[6][axis]
+    bl, bu = wl * normal, wu * normal
+
+    def carried(one, two):
+        return al * one + au * two
+
+    others = [c for c in range(3) if c != axis]
+    result = [carried(lower[2][0], upper[2][0])]
+    for c in range(3):
+        value = carried(lower[2][1 + c], upper[2][1 + c])
+        if c == axis:
+            value = value + (wl * lower[3] + wu * upper[3])
+        else:
+            value = value - (bl * lower[6][c] + bu * upper[6][c])
+        result.append(value)
+    result.append(carried(lower[2][4], upper[2][4]) + (wl * lower[4] + wu * upper[4]))
+    for c in others:
+        result.append(
+            carried(lower[6][c], upper[6][c]) - (bl * lower[5][c] + bu * upper[5][c])
+        )
+    return result
 
 
 def kernel(
     sizes, rho_hbm, vel_hbm, pre_hbm, fld_hbm, corona_hbm, res,
-    stack, raw, marks, sbuf, rbuf, pad, ext, xsend, xrecv, part, load_sem, send_sem, recv_sem, ready,
+    stack, raw, marks, sbuf, rbuf, pad, ext, xsend, xrecv, part, load_sem, send_sem, recv_sem,
 ):
     nz, ny, nx, gz, gy, gx = sizes
     plane = nz * ny
@@ -116,7 +128,7 @@
     barrier = pltpu.get_barrier_semaphore()
     for to in (left, right):
         pl.semaphore_signal(barrier, inc=1, device_id={"gx": to}, device_id_type=MESH)
-    for dz, dy in DIRS[:4]:
+    for dz, dy in DIRS:
         @pl.when(exists(dz, dy))
         def _():
             pl.semaphore_signal(
@@ -181,13 +193,8 @@
 
     pl.semaphore_wait(
         barrier,
-        2 + sum(exists(dz, dy).astype(jnp.int32) for dz, dy in DIRS[:4]),
+        2 + sum(exists(dz, dy).astype(jnp.int32) for dz, dy in DIRS),
     )
-
-    for dz in (-1, 1):
-        @pl.when(has_z[dz])
-        def _():
-            pl.semaphore_signal(ready, inc=1, device_id={"gz": iz + dz}, device_id_type=MESH)
 
     def message(d):
         dz, dy = DIRS[d]
@@ -201,9 +208,6 @@
         )
 
     for d in range(8):
-        if d == 4:
-            pl.semaphore_wait(ready, has_z[-1].astype(jnp.int32) + has_z[1].astype(jnp.int32))
-
         @pl.when(exists(*DIRS[d]))
         def _():
             message(d).start()
@@ -334,7 +338,7 @@
             umag = [faces[c] if c == axis else centre[c] for c in range(3)]
             lower = state_terms(lcell, lvel, lpre, lmag, axis)
             upper = state_terms(cell, vel, pre, umag, axis)
-            fluxes.append(hll(lower, upper))
+            fluxes.append(hll(lower, upper, axis))
         squared = centre[0] * centre[0] + centre[1] * centre[1] + centre[2] * centre[2]
         base = [rho] + list(cell[4]) + [cell[3] + 0.5 * squared]
         fz, fy, fx = fluxes
@@ -355,16 +359,11 @@
         part[14, out, :] = fy[6]
 
     count = nx // 8
-    for k in range(1, count):
+    def body(k, carry):
         chunk(k)
-    to_left.wait_recv()
-    to_right.wait_recv()
-    ext[pl.ds(8 + nx, FIELDS, stride=tall), :] = xrecv[pl.ds(0, FIELDS), :]
-    ext[pl.ds(FX * tall + 9 + nx, 1), :] = xrecv[pl.ds(FIELDS, 1), :]
-    ext[pl.ds(7, FIELDS, stride=tall), :] = xrecv[pl.ds(16, FIELDS), :]
-    chunk(0)
-    chunk(count)
-
+        return carry
+
+    lax.fori_loop(1, count, body, 0, unroll=3)
     def finish(k):
         at = 8 * k
         here, after, before = pl.ds(at + 1, 8), pl.ds(at + 2, 8), pl.ds(at, 8)
@@ -379,8 +378,18 @@
         res[6, before, :] = ext[pl.ds(FY * tall + at + 8, 8), :] - courant * ((up(ex, 0) - ex) - (ez_next - ez))
         res[5, before, :] = ext[pl.ds(FZ * tall + at + 8, 8), :] - courant * ((ey_next - ey) - (up(ex, 1) - ex))
 
-    for k in range(count):
+    for k in range(1, count - 1):
         finish(k)
+    to_left.wait_recv()
+    to_right.wait_recv()
+    ext[pl.ds(8 + nx, FIELDS, stride=tall), :] = xrecv[pl.ds(0, FIELDS), :]
+    ext[pl.ds(FX * tall + 9 + nx, 1), :] = xrecv[pl.ds(FIELDS, 1), :]
+    ext[pl.ds(7, FIELDS, stride=tall), :] = xrecv[pl.ds(16, FIELDS), :]
+    chunk(0)
+    chunk(count)
+
+    finish(0)
+    finish(count - 1)
     for d in range(8):
         @pl.when(exists(*DIRS[d]))
         def _():
@@ -433,7 +442,6 @@
             pltpu.SemaphoreType.DMA((5,)),
             pltpu.SemaphoreType.DMA((10,)),
             pltpu.SemaphoreType.DMA((10,)),
-            pltpu.SemaphoreType.REGULAR,
         ],
         compiler_params=pltpu.CompilerParams(
             collective_id=0, has_side_effects=True, vmem_limit_bytes=16 << 20

time: 13 us -> 12.7 us (0.977)
  the two profiles are of different devices: /device:TPU:0 before, /device:TPU:1 now
where the time goes in v4:
time: 12.7 us; the launch traced here: 12.5 us
  Pallas kernels  11.9 us (94%)
  between operations  0.64 us (5%)
    pallas_call x1, Pallas kernels, on_device(): pl.pallas_call(functools.partial(kernel, (nz, ny, nx, gz, gy, gx)), out_s...  11 us
    pallas_call x1, Pallas kernels, on_device(): pl.pallas_call(functools.partial(unpack_kernel, (nz, ny)), out_shape=(jax...  0.93 us

profile of v4, /device:TPU:1, one launch (start us, length us, event | category | flops | bytes accessed | tf_op | source)
XLA Modules:
  0.0 12.5 jit_solution(3897220009217497885)
XLA Ops:
  0.6 11.0 %shard_map.68.res = f32[8,128,128]{2,1,0:T(8,128)S(1)} custom-call(f32[64,128]{1,0:T(8,128)} %bitcast.8, f32[192,128]{1,0:T(8,128)} %bitcast.6, f32[64,128]{1,0:T(8,128)} %bitcast.9, f32[192,128]{1,0:T(8,128)} %bitcast.7, s32[16]{0:T(128)} %corona_hbm.1), custom_call_target="tpu_custom_call" | custom-call | tf_op jit(solution)/shard_map/pallas_call | solution.py:426
  11.6 0.9 %shard_map.69 = (f32[320,128]{1,0:T(8,128)}, f32[192,128]{1,0:T(8,128)}) custom-call(f32[8,128,128]{2,1,0:T(8,128)S(1)} %shard_map.68.res), custom_call_target="tpu_custom_call" | custom-call | tf_op jit(solution)/shard_map/pallas_call | solution.py:461
